TPU v7x, 32 devices: a whole 2x2x4 slice. The times are simulated.
32 devices in a mesh: row: 4 (over z), col: 8 (over y, x, core).
Axes of the slice: x: 2, y: 2, z: 4, core: 2. Of those that a mesh axis runs over, the one named last changes fastest.
Arguments:
- dec_src: float32 [2304, 8192], P('col', 'row'), may hold values from -6 to 6
- enc_tgt: float32 [2304, 16384], P('row', 'col'), may hold values from -0.125 to 0.125
- src_coacts: float32 [512, 8192], P('col', 'row'), may hold values from -6 to 6
- tgt_coacts: float32 [512, 16384], P('row', 'col'), may hold values from -6 to 6
- eval_src: float32 [512, 8192], P('col', 'row'), may hold values from -6 to 6
- enc_bias: float32 [16384], P('col'), may hold values from -0.5 to 0.5
- dec_tgt: float32 [2304, 16384], P('row', 'col'), may hold values from -0.046875 to 0.046875
- tile_mask: int32 [128, 256], P('row', 'col'), may hold values from 0 to 1, as said below
Outputs:
- recon: float32 [512, 2304], P('col', 'row')
Inputs may be any that keep to these rules, and one draw needn't show every extreme that they name: `tile_mask`: 1 keeps a tile, 0 prunes it; the share of kept tiles differs between regions of the grid.
All inputs are finite; a program needn't handle non-finite values.
Results may differ from a plain program's by a relative error of at most 0.0003.
Values sent between devices are 32-bit elements; how exact they have to be, the bound alone decides.
A program may use at most 192 MiB of HBM per device.

v0:
```python
import jax
import jax.numpy as jnp
from jax import lax
from jax.sharding import PartitionSpec as P

S = 8192
TILE = 64
PRECISE = lax.Precision.HIGHEST


def contract_first(left, right):
    return lax.dot_general(
        left, right, (((0,), (0,)), ((), ())), precision=PRECISE, preferred_element_type=jnp.float32
    )


def local(dec_src, enc_tgt, src_coacts, tgt_coacts, eval_src, enc_bias, dec_tgt, tile_mask):
    src_count = dec_src.shape[1]
    tgt_count = enc_tgt.shape[1]
    enc_full = lax.all_gather(enc_tgt, "row", axis=0, tiled=True)
    src_full, eval_full = (
        lax.all_gather(src_coacts, "col", axis=0, tiled=True),
        lax.all_gather(eval_src, "col", axis=0, tiled=True),
    )
    virtual = contract_first(lax.all_gather(dec_src, "col", axis=0, tiled=True), enc_full)
    coact = contract_first(src_full, lax.all_gather(tgt_coacts, "row", axis=0, tiled=True))
    coact = coact * (1.0 / jnp.sqrt(jnp.float32(src_full.shape[0])))
    tile_rows, tile_cols = tile_mask.shape
    mask_float = tile_mask.astype(jnp.float32)
    weighted = (
        (virtual * coact).reshape(tile_rows, TILE, tile_cols, TILE) * mask_float[:, None, :, None]
    ).reshape(src_count, tgt_count)
    partial_pre = jnp.dot(
        eval_full, weighted, precision=PRECISE, preferred_element_type=jnp.float32
    )
    scale = 1.0 / jnp.sqrt(jnp.float32(S))
    pre_acts = lax.psum(partial_pre, "row")
    hidden = jnp.maximum(pre_acts * scale + enc_bias[None, :], 0.0)
    recon_part = lax.dot_general(
        hidden,
        dec_tgt,
        (((1,), (1,)), ((), ())),
        precision=PRECISE,
        preferred_element_type=jnp.float32,
    )
    return lax.psum_scatter(recon_part, "col", scatter_dimension=0, tiled=True)


def solution(mesh):
    return jax.shard_map(
        local,
        mesh=mesh,
        in_specs=(
            P("col", "row"),
            P("row", "col"),
            P("col", "row"),
            P("row", "col"),
            P("col", "row"),
            P("col"),
            P("row", "col"),
            P("row", "col"),
        ),
        out_specs=P("col", "row"),
        check_vma=False,
    )
```

profile of v0, /device:TPU:0, one launch (start us, length us, event | category | flops | bytes accessed | tf_op | source)
XLA Modules:
  0.0 963.4 jit_solution(13110801990855593298)
XLA Ops:
  6.5 0.0 copy-start
  6.5 0.0 all-gather.12.cloned.1.call-start
  6.5 0.7 all-gather.12.cloned.1.call-update
  7.3 0.0 all-gather.10.cloned.1.call-start
  7.3 0.7 all-gather.10.cloned.1.call-update
  8.0 0.0 all-gather.8.cloned.1.call-start
  8.1 0.7 all-gather.8.cloned.1.call-update
  8.7 0.0 all-gather.6.cloned.1.call-start
  8.8 0.5 all-gather.6.cloned.1.call-update
  9.3 0.0 all-gather.14.cloned.1.call-start
  9.4 0.5 all-gather.14.cloned.1.call-update
  9.9 0.0 all-reduce.2.cloned.1.call-start
  10.0 0.0 copy-done
  10.0 11.9 %mul.29 = f32[32,64,32,64]{3,2,1,0:T(8,128)} broadcast(f32[32,32]{1,0:T(8,128)S(1)} %convert_element_type.3), dimensions={0,2} | broadcast | bytes 16781312 | tf_op jit(solution)/shard_map/mul | solution.py:31
  21.9 29.0 %mul.30 = f32[2048,2048]{1,0:T(8,128)} reshape(f32[32,64,32,64]{3,2,1,0:T(8,128)} %mul.29) | data formatting | bytes 33554432 | tf_op jit(solution)/shard_map/mul | solution.py:31
  50.9 41.5 %all-gather.12.cloned.1.call-done = f32[512,2048]{1,0:T(8,128)} async-done(((f32[128,2048]{1,0:T(8,128)}), f32[512,2048]{1,0:T(8,128)}) %all-gather.12.cloned.1.call-update) | async-done | bytes 4194320 | tf_op jit(solution)/shard_map/all_gather | solution.py:26
  92.4 37.0 %all-gather.10.cloned.1.call-done = f32[512,2048]{1,0:T(8,128)} async-done(((f32[64,2048]{1,0:T(8,128)}), f32[512,2048]{1,0:T(8,128)}) %all-gather.10.cloned.1.call-update) | async-done | bytes 4194320 | tf_op jit(solution)/shard_map/all_gather | solution.py:22
  129.4 31.4 %fusion.19 = f32[2048,2048]{1,0:T(8,128)} fusion(f32[512,2048]{1,0:T(8,128)} %all-gather.10.cloned.1.call-done, f32[512,2048]{1,0:T(8,128)} %all-gather.12.cloned.1.call-done), kind=kOutput, calls=%fused_computation.17 | convolution fusion | flops 25769803776 | bytes 25165824 | tf_op jit(solution)/shard_map/dot_general | solution.py:12
  160.8 292.8 %all-gather.8.cloned.1.call-done = f32[2304,2048]{1,0:T(8,128)} async-done(((f32[576,2048]{1,0:T(8,128)}), f32[2304,2048]{1,0:T(8,128)}) %all-gather.8.cloned.1.call-update) | async-done | bytes 18874384 | tf_op jit(solution)/shard_map/all_gather | solution.py:20
  453.6 99.2 %all-gather.6.cloned.1.call-done = f32[2304,2048]{1,0:T(8,128)} async-done(((f32[288,2048]{1,0:T(8,128)}), f32[2304,2048]{1,0:T(8,128)}) %all-gather.6.cloned.1.call-update) | async-done | bytes 18874384 | tf_op jit(solution)/shard_map/all_gather | solution.py:25
  552.8 125.5 %fusion.18 = f32[2048,2048]{1,0:T(8,128)} fusion(f32[2304,2048]{1,0:T(8,128)} %all-gather.6.cloned.1.call-done, f32[2304,2048]{1,0:T(8,128)} %all-gather.8.cloned.1.call-done), kind=kOutput, calls=%fused_computation.16 | convolution fusion | flops 115964116992 | bytes 54525952 | tf_op jit(solution)/shard_map/dot_general | solution.py:12
  678.3 0.0 copy-start.1
  678.3 0.0 all-gather.14.cloned.1.call-done
  678.4 62.9 %fusion.9 = f32[512,2048]{0,1:T(8,128)} fusion(f32[512,2048]{1,0:T(8,128)} %all-gather.14.cloned.1.call-done, f32[2048,2048]{1,0:T(8,128)} %mul.30, f32[2048,2048]{1,0:T(8,128)} %fusion.18, f32[2048,2048]{1,0:T(8,128)} %fusion.19), kind=kOutput, calls=%fused_computation.9 | convolution fusion | flops 25782386688 | bytes 58720256 | tf_op jit(solution)/shard_map/dot_general | solution.py:33
  741.2 0.0 all-reduce.2.cloned.1.call-update
  741.3 0.0 reduce-scatter.2.cloned.1.call-start
  741.3 155.1 %all-reduce.2.cloned.1.call-done = f32[512,2048]{0,1:T(8,128)} async-done(((f32[512,2048]{0,1:T(8,128)}), f32[512,2048]{0,1:T(8,128)}) %all-reduce.2.cloned.1.call-update) | async-done | bytes 4194320 | tf_op jit(solution)/shard_map/psum | solution.py:37
  896.4 0.0 copy-done.1
  896.4 23.6 %fusion.5 = f32[512,576]{1,0:T(8,128)} fusion(f32[576,2048]{1,0:T(8,128)} %param.14, f32[512,2048]{0,1:T(8,128)} %all-reduce.2.cloned.1.call-done, f32[2048]{0:T(1024)S(1)} %copy-done.1), kind=kOutput, calls=%fused_computation.5 | convolution fusion | flops 7250903040 | bytes 10100736 | tf_op jit(solution)/shard_map/dot_general | solution.py:39
  920.1 0.0 reduce-scatter.2.cloned.1.call-update
  920.1 36.3 %reduce-scatter.2.cloned.1.call-done = f32[64,576]{1,0:T(8,128)} async-done(((f32[512,576]{1,0:T(8,128)}), f32[64,576]{1,0:T(8,128)}) %reduce-scatter.2.cloned.1.call-update) | async-done | bytes 147472 | tf_op jit(solution)/shard_map/reduce_scatter | solution.py:46
  (1 shorter events, 0.0 us)
Async XLA Ops:
  6.5 3.4 copy-start
  6.5 85.9 %all-gather.12.cloned.1.call-start = ((), (), s32[]{:S(2)}) async-start(), calls=%async_computation.4 | async-start | bytes 5242880 | tf_op jit(solution)/shard_map/all_gather | solution.py:26
  7.3 122.1 %all-gather.10.cloned.1.call-start = ((), (), s32[]{:S(2)}) async-start(), calls=%async_computation.3 | async-start | bytes 4718592 | tf_op jit(solution)/shard_map/all_gather | solution.py:22
  8.0 445.6 %all-gather.8.cloned.1.call-start = ((), (), s32[]{:S(2)}) async-start(), calls=%async_computation.2 | async-start | bytes 23592960 | tf_op jit(solution)/shard_map/all_gather | solution.py:20
  8.7 544.0 %all-gather.6.cloned.1.call-start = ((), (), s32[]{:S(2)}) async-start(), calls=%async_computation.1 | async-start | bytes 21233664 | tf_op jit(solution)/shard_map/all_gather | solution.py:25
  9.3 669.0 %all-gather.14.cloned.1.call-start = ((), (), s32[]{:S(2)}) async-start(), calls=%async_computation.5 | async-start | bytes 4718592 | tf_op jit(solution)/shard_map/all_gather | solution.py:23
  9.9 886.5 %all-reduce.2.cloned.1.call-start = ((), (), s32[]{:S(2)}) async-start(), calls=%async_computation.6 | async-start | bytes 8388608 | tf_op jit(solution)/shard_map/psum | solution.py:37
  678.3 218.1 %copy-start.1 = (f32[2048]{0:T(1024)S(1)}, f32[2048]{0:T(1024)}, u32[]{:S(2)}) copy-start(f32[2048]{0:T(1024)} %param.13) | copy-start | bytes 24580
  741.3 215.1 %reduce-scatter.2.cloned.1.call-start = ((), (), s32[]{:S(2)}) async-start(), calls=%async_computation.7 | async-start | bytes 1474560 | tf_op jit(solution)/shard_map/reduce_scatter | solution.py:46
Sparse Core Ops, SparseCore 0:
  8.9 83.4 all-gather.11
  94.3 35.0 all-gather.9
  131.0 322.5 all-gather.7
  455.3 97.4 all-gather.5
  554.5 36.5 all-gather.13
  741.4 154.9 all-reduce.1
  920.2 36.1 reduce-scatter.1
where the time goes:
time: 970 us; the launch traced here: 963 us
  waiting for transfers between devices  665 us (69%)
  matrix products  243 us (25%)
  local copies, waits for them, and re-layouts  40.9 us (4%)
  between operations  13.7 us (1%)
    all_gather x1, waiting for transfers between devices, local(): enc_full = lax.all_gather(enc_tgt, 'row', axis=0, tiled=True)  293 us
    dot_general x2, matrix products, contract_first(): lax.dot_general(left, right, (((0,), (0,)), ((), ())), precision=PRECISE,...  157 us
    psum x1, waiting for transfers between devices, local(): pre_acts = lax.psum(partial_pre, 'row')  155 us
    all_gather x1, waiting for transfers between devices, local(): lax.all_gather(dec_src, 'col', axis=0, tiled=True)  99.2 us
    dot_general x1, matrix products, local(): jnp.dot(eval_full, weighted, precision=PRECISE, preferred_element_type=jn...  62.9 us
    all_gather x1, waiting for transfers between devices, local(): lax.all_gather(tgt_coacts, 'row', axis=0, tiled=True)  41.5 us
    mul x2, local copies, waits for them, and re-layouts, local(): (virtual * coact).reshape(tile_rows, TILE, tile_cols, TILE)  40.9 us
    all_gather x1, waiting for transfers between devices, local(): lax.all_gather(src_coacts, 'col', axis=0, tiled=True)  37 us
  transfers between devices with their start and end apart: 7, of which 6 were waited for; matrix products, arithmetic and copies ran while one was open for 21% of the time, Pallas kernels for 0%

commit v1 on v0

--- a/solution.py
+++ b/solution.py
@@ -34,7 +34,7 @@
         eval_full, weighted, precision=PRECISE, preferred_element_type=jnp.float32
     )
     scale = 1.0 / jnp.sqrt(jnp.float32(S))
-    pre_acts = lax.psum(partial_pre, "row")
+    pre_acts = jax.lax.all_gather(partial_pre, "row").sum(axis=0)
     hidden = jnp.maximum(pre_acts * scale + enc_bias[None, :], 0.0)
     recon_part = lax.dot_general(
         hidden,

time: 970 us -> 1140 us (1.18)
  waiting for transfers between devices: 665 us -> 796 us
  local copies, waits for them, and re-layouts: 40.9 us -> 61.3 us
  other arithmetic: 0.01 us -> 16.1 us
    all_gather x0 -> x1, waiting for transfers between devices: none -> 287 us  [local(): pre_acts = jax.lax.all_gather(partial_pre, 'row').sum(axis=0)]
    psum x1 -> x0, waiting for transfers between devices: 155 us -> none  [local(): pre_acts = lax.psum(partial_pre, 'row')]
    all_gather x0 -> x1, local copies, waits for them, and re-layouts: none -> 20.4 us  [local(): pre_acts = jax.lax.all_gather(partial_pre, 'row').sum(axis=0)]
    reduce_sum x0 -> x1, other arithmetic: none -> 16.1 us  [local(): pre_acts = jax.lax.all_gather(partial_pre, 'row').sum(axis=0)]
  transfers between devices with their start and end apart: 7 -> 7, of which waited for: 6 -> 6; matrix products, arithmetic and copies ran while one was open for 21% -> 17% of each run, Pallas kernels for 0% -> 0%
where the time goes in v1:
time: 1140 us; the launch traced here: 1130 us
  waiting for transfers between devices  796 us (70%)
  matrix products  243 us (21%)
  local copies, waits for them, and re-layouts  61.3 us (5%)
  other arithmetic  16.1 us (1%)
  between operations  13.7 us (1%)
    all_gather x1, waiting for transfers between devices, local(): enc_full = lax.all_gather(enc_tgt, 'row', axis=0, tiled=True)  293 us
    all_gather x1, waiting for transfers between devices, local(): pre_acts = jax.lax.all_gather(partial_pre, 'row').sum(axis=0)  287 us
    dot_general x2, matrix products, contract_first(): lax.dot_general(left, right, (((0,), (0,)), ((), ())), precision=PRECISE,...  157 us
    all_gather x1, waiting for transfers between devices, local(): lax.all_gather(dec_src, 'col', axis=0, tiled=True)  99.2 us
    dot_general x1, matrix products, local(): jnp.dot(eval_full, weighted, precision=PRECISE, preferred_element_type=jn...  62.9 us
    all_gather x1, waiting for transfers between devices, local(): lax.all_gather(tgt_coacts, 'row', axis=0, tiled=True)  41.5 us
    mul x2, local copies, waits for them, and re-layouts, local(): (virtual * coact).reshape(tile_rows, TILE, tile_cols, TILE)  40.9 us
    all_gather x1, waiting for transfers between devices, local(): lax.all_gather(src_coacts, 'col', axis=0, tiled=True)  37 us
  transfers between devices with their start and end apart: 7, of which 6 were waited for; matrix products, arithmetic and copies ran while one was open for 17% of the time, Pallas kernels for 0%

profile of v1, /device:TPU:0, one launch (start us, length us, event | category | flops | bytes accessed | tf_op | source)
XLA Modules:
  0.0 1130.9 jit_solution(6221076987516872284)
XLA Ops:
  6.5 0.0 copy-start
  6.5 0.0 all-gather.14.cloned.1.call-start
  6.5 0.7 all-gather.14.cloned.1.call-update
  7.3 0.0 all-gather.12.cloned.1.call-start
  7.3 0.7 all-gather.12.cloned.1.call-update
  8.0 0.0 all-gather.10.cloned.1.call-start
  8.1 0.7 all-gather.10.cloned.1.call-update
  8.7 0.0 all-gather.8.cloned.1.call-start
  8.8 0.5 all-gather.8.cloned.1.call-update
  9.3 0.0 all-gather.16.cloned.1.call-start
  9.4 0.5 all-gather.16.cloned.1.call-update
  9.9 0.0 all-gather.18.cloned.1.call-start
  10.0 0.0 copy-done
  10.0 11.9 %mul.29 = f32[32,64,32,64]{3,2,1,0:T(8,128)} broadcast(f32[32,32]{1,0:T(8,128)S(1)} %convert_element_type.3), dimensions={0,2} | broadcast | bytes 16781312 | tf_op jit(solution)/shard_map/mul | solution.py:31
  21.9 29.0 %mul.30 = f32[2048,2048]{1,0:T(8,128)} reshape(f32[32,64,32,64]{3,2,1,0:T(8,128)} %mul.29) | data formatting | bytes 33554432 | tf_op jit(solution)/shard_map/mul | solution.py:31
  50.9 41.5 %all-gather.14.cloned.1.call-done = f32[512,2048]{1,0:T(8,128)} async-done(((f32[128,2048]{1,0:T(8,128)}), f32[512,2048]{1,0:T(8,128)}) %all-gather.14.cloned.1.call-update) | async-done | bytes 4194320 | tf_op jit(solution)/shard_map/all_gather | solution.py:26
  92.4 37.0 %all-gather.12.cloned.1.call-done = f32[512,2048]{1,0:T(8,128)} async-done(((f32[64,2048]{1,0:T(8,128)}), f32[512,2048]{1,0:T(8,128)}) %all-gather.12.cloned.1.call-update) | async-done | bytes 4194320 | tf_op jit(solution)/shard_map/all_gather | solution.py:22
  129.4 31.4 %fusion.19 = f32[2048,2048]{1,0:T(8,128)} fusion(f32[512,2048]{1,0:T(8,128)} %all-gather.12.cloned.1.call-done, f32[512,2048]{1,0:T(8,128)} %all-gather.14.cloned.1.call-done), kind=kOutput, calls=%fused_computation.17 | convolution fusion | flops 25769803776 | bytes 25165824 | tf_op jit(solution)/shard_map/dot_general | solution.py:12
  160.8 292.8 %all-gather.10.cloned.1.call-done = f32[2304,2048]{1,0:T(8,128)} async-done(((f32[576,2048]{1,0:T(8,128)}), f32[2304,2048]{1,0:T(8,128)}) %all-gather.10.cloned.1.call-update) | async-done | bytes 18874384 | tf_op jit(solution)/shard_map/all_gather | solution.py:20
  453.6 99.2 %all-gather.8.cloned.1.call-done = f32[2304,2048]{1,0:T(8,128)} async-done(((f32[288,2048]{1,0:T(8,128)}), f32[2304,2048]{1,0:T(8,128)}) %all-gather.8.cloned.1.call-update) | async-done | bytes 18874384 | tf_op jit(solution)/shard_map/all_gather | solution.py:25
  552.8 125.5 %fusion.18 = f32[2048,2048]{1,0:T(8,128)} fusion(f32[2304,2048]{1,0:T(8,128)} %all-gather.8.cloned.1.call-done, f32[2304,2048]{1,0:T(8,128)} %all-gather.10.cloned.1.call-done), kind=kOutput, calls=%fused_computation.16 | convolution fusion | flops 115964116992 | bytes 54525952 | tf_op jit(solution)/shard_map/dot_general | solution.py:12
  678.3 0.0 all-gather.16.cloned.1.call-done
  678.3 62.9 %fusion.9 = f32[512,2048]{0,1:T(8,128)} fusion(f32[512,2048]{1,0:T(8,128)} %all-gather.16.cloned.1.call-done, f32[2048,2048]{1,0:T(8,128)} %mul.30, f32[2048,2048]{1,0:T(8,128)} %fusion.18, f32[2048,2048]{1,0:T(8,128)} %fusion.19), kind=kOutput, calls=%fused_computation.9 | convolution fusion | flops 25782386688 | bytes 58720256 | tf_op jit(solution)/shard_map/dot_general | solution.py:33
  741.2 0.0 all-gather.18.cloned.1.call-update
  741.2 0.0 reduce-scatter.2.cloned.1.call-start
  741.3 286.9 %all-gather.18.cloned.1.call-done = f32[2048,2048]{0,1:T(8,128)} async-done(((f32[512,2048]{0,1:T(8,128)}), f32[2048,2048]{0,1:T(8,128)}) %all-gather.18.cloned.1.call-update) | async-done | bytes 16777232 | tf_op jit(solution)/shard_map/all_gather | solution.py:37
  1028.2 20.4 %reshape.5 = f32[4,512,2048]{1,0,2:T(4,128)} reshape(f32[2048,2048]{0,1:T(8,128)} %all-gather.18.cloned.1.call-done) | data formatting | bytes 33554432 | tf_op jit(solution)/shard_map/all_gather | solution.py:37
  1048.6 16.1 %reduce_sum.9 = f32[512,2048]{0,1:T(8,128)} reduce(f32[4,512,2048]{1,0,2:T(4,128)} %reshape.5, f32[]{:T(128)} %constant.0.clone.1), dimensions={0}, to_apply=%region_0.0 | reduce | flops 3145728 | bytes 20971524 | tf_op jit(solution)/shard_map/reduce_sum | solution.py:37
  1064.7 0.0 copy-done.1
  1064.7 23.6 %fusion.5 = f32[512,576]{1,0:T(8,128)} fusion(f32[576,2048]{1,0:T(8,128)} %param.14, f32[512,2048]{0,1:T(8,128)} %reduce_sum.9, f32[2048]{0:T(1024)S(1)} %copy-done.1), kind=kOutput, calls=%fused_computation.5 | convolution fusion | flops 7250903040 | bytes 10100736 | tf_op jit(solution)/shard_map/dot_general | solution.py:39
  1088.3 0.0 reduce-scatter.2.cloned.1.call-update
  1088.3 35.5 %reduce-scatter.2.cloned.1.call-done = f32[64,576]{1,0:T(8,128)} async-done(((f32[512,576]{1,0:T(8,128)}), f32[64,576]{1,0:T(8,128)}) %reduce-scatter.2.cloned.1.call-update) | async-done | bytes 147472 | tf_op jit(solution)/shard_map/reduce_scatter | solution.py:46
  (2 shorter events, 0.0 us)
Async XLA Ops:
  6.5 3.4 copy-start
  6.5 85.9 %all-gather.14.cloned.1.call-start = ((), (), s32[]{:S(2)}) async-start(), calls=%async_computation.4 | async-start | bytes 5242880 | tf_op jit(solution)/shard_map/all_gather | solution.py:26
  7.3 122.1 %all-gather.12.cloned.1.call-start = ((), (), s32[]{:S(2)}) async-start(), calls=%async_computation.3 | async-start | bytes 4718592 | tf_op jit(solution)/shard_map/all_gather | solution.py:22
  8.0 445.6 %all-gather.10.cloned.1.call-start = ((), (), s32[]{:S(2)}) async-start(), calls=%async_computation.2 | async-start | bytes 23592960 | tf_op jit(solution)/shard_map/all_gather | solution.py:20
  8.7 544.1 %all-gather.8.cloned.1.call-start = ((), (), s32[]{:S(2)}) async-start(), calls=%async_computation.1 | async-start | bytes 21233664 | tf_op jit(solution)/shard_map/all_gather | solution.py:25
  9.3 669.0 %all-gather.16.cloned.1.call-start = ((), (), s32[]{:S(2)}) async-start(), calls=%async_computation.5 | async-start | bytes 4718592 | tf_op jit(solution)/shard_map/all_gather | solution.py:23
  9.9 1018.2 %all-gather.18.cloned.1.call-start = ((), (), s32[]{:S(2)}) async-start(), calls=%async_computation.7 | async-start | bytes 20971520 | tf_op jit(solution)/shard_map/all_gather | solution.py:37
  741.2 382.6 %reduce-scatter.2.cloned.1.call-start = ((), (), s32[]{:S(2)}) async-start(), calls=%async_computation.6 | async-start | bytes 1474560 | tf_op jit(solution)/shard_map/reduce_scatter | solution.py:46
  1048.6 16.1 %copy-start.1 = (f32[2048]{0:T(1024)S(1)}, f32[2048]{0:T(1024)}, u32[]{:S(2)}) copy-start(f32[2048]{0:T(1024)} %param.13) | copy-start | bytes 24580
Sparse Core Ops, SparseCore 0:
  8.9 83.4 all-gather.13
  94.3 35.0 all-gather.11
  131.0 322.5 all-gather.9
  455.3 97.4 all-gather.7
  554.5 36.5 all-gather.15
  741.4 286.7 all-gather.17
  1088.5 35.3 reduce-scatter.1
